TPU v7x, 32 devices: a whole 2x2x4 slice. The times are simulated.
32 devices in a mesh: dp: 8 (over z, x), tensor: 4 (over y, core).
Axes of the slice: x: 2, y: 2, z: 4, core: 2. Of those that a mesh axis runs over, the one named last changes fastest.
Arguments:
- tokens: bfloat16 [25088, 768], P(('dp', 'tensor')), may hold values from -6 to 6
- cotangent: bfloat16 [25088, 768], P(('dp', 'tensor')), may hold values from -6 to 6
- block_patches: int32 [32], P('dp'), may hold values from 196 to 784, as said below
- qkv_weight: bfloat16 [3, 768, 768], P(None, 'dp', 'tensor'), may hold values from -0.21875 to 0.21875
- out_weight: bfloat16 [768, 768], P('tensor', 'dp'), may hold values from -0.875 to 0.875
- up_weight: bfloat16 [768, 3072], P('dp', 'tensor'), may hold values from -0.21875 to 0.21875
- down_weight: bfloat16 [3072, 768], P('tensor', 'dp'), may hold values from -0.109375 to 0.109375
- vectors: float32 [9216], replicated, may hold values from -0.7 to 1.7, as said below
- momentum: float32 [1], replicated, may hold values from 0.4 to 0.7
- target_qkv: float32 [3, 768, 768], P(None, 'dp', 'tensor'), may hold values from -0.21875 to 0.21875
- target_out: float32 [768, 768], P('tensor', 'dp'), may hold values from -0.875 to 0.875
- target_up: float32 [768, 3072], P('dp', 'tensor'), may hold values from -0.21875 to 0.21875
- target_down: float32 [3072, 768], P('tensor', 'dp'), may hold values from -0.109375 to 0.109375
- target_vectors: float32 [9216], replicated, may hold values from -0.7 to 1.7, as said below
Outputs:
- output: bfloat16 [25088, 768], P(('dp', 'tensor'))
- grad_tokens: bfloat16 [25088, 768], P(('dp', 'tensor'))
- grad_qkv: float32 [3, 768, 768], P(None, 'dp', 'tensor')
- grad_out: float32 [768, 768], P('tensor', 'dp')
- grad_up: float32 [768, 3072], P('dp', 'tensor')
- grad_down: float32 [3072, 768], P('tensor', 'dp')
- grad_vectors: float32 [9216], replicated
- next_qkv: float32 [3, 768, 768], P(None, 'dp', 'tensor')
- next_out: float32 [768, 768], P('tensor', 'dp')
- next_up: float32 [768, 3072], P('dp', 'tensor')
- next_down: float32 [3072, 768], P('tensor', 'dp')
- next_vectors: float32 [9216], replicated
Inputs may be any that keep to these rules, and one draw needn't show every extreme that they name: `block_patches`: each block of 784 rows holds either one image of 784 patches (entry 784) or four images of 196 patches, one after another (entry 196); both kinds occur in every draw. `vectors`: the gains (the first and third pieces of 768) lie between 0.3 and 1.7. `target_vectors`: laid out as vectors, with gains between 0.3 and 1.7.
All inputs are finite; a program needn't handle non-finite values.
Results may differ from a plain program's by a relative error of at most 0.012.
Values may be sent and summed in bfloat16 or wider, within the bound.
A program may use at most 192 MiB of HBM per device.

v0:
```python
import jax
import jax.numpy as jnp
from jax import lax
from jax.sharding import PartitionSpec as P

HD = 64
BOTH = ("dp", "tensor")
F32 = jnp.float32
BF16 = jnp.bfloat16


def unpack(vectors, d, ff):
    cuts = [d * i for i in range(8)] + [7 * d + ff, 8 * d + ff]
    return tuple((vectors[a:b] for a, b in zip(cuts[:-1], cuts[1:])))


def norm_parts(values):
    centred = values - jnp.mean(values, axis=-1, keepdims=True)
    inverse = lax.rsqrt(jnp.mean(centred * centred, axis=-1, keepdims=True) + 1e-06)
    return (centred * inverse, inverse)


def norm_backward(grad_normed, scaled, inverse, gain):
    weighted = grad_normed * gain
    return inverse * (
        weighted
        - jnp.mean(weighted, axis=-1, keepdims=True)
        - scaled * jnp.mean(weighted * scaled, axis=-1, keepdims=True)
    )


def gelu_parts(v):
    cdf = 0.5 * (1.0 + lax.erf(v * 0.5**0.5))
    return (v * cdf, cdf + v * jnp.exp(-0.5 * v * v) * (2.0 * jnp.pi) ** (-0.5))


def dot(a, b, dims):
    return lax.dot_general(a, b, (dims, ((), ())), preferred_element_type=F32)


def pack_shards(qkv, out, up, down):
    first = jnp.concatenate([qkv[0], qkv[1], qkv[2], out.T], axis=1)
    return jnp.stack([first, up, down.T])


def gather_blocks(shards, dp, tensor):
    every = lax.all_gather(shards, BOTH, axis=0)
    b, r, c = shards.shape
    every = every.reshape(dp, tensor, b, r, c).transpose(2, 1, 0, 3, 4)
    return every.reshape(b, tensor, dp * r, c)


def scatter_blocks(blocks, dp, tensor):
    b, t, rows, c = blocks.shape
    r = rows // dp
    pieces = blocks.reshape(b, tensor, dp, r, c).transpose(2, 1, 0, 3, 4)
    pieces = pieces.reshape(dp * tensor, b, r, c)
    return lax.psum_scatter(pieces, BOTH, scatter_dimension=0, tiled=True)[0]


def local_layer(tokens, cotangent, patches, blocks, vectors):
    rows, d = tokens.shape
    tensor, c = (blocks.shape[1], blocks.shape[3])
    w = c // 4
    ff = tensor * c
    heads = d // HD
    gain1, bias1, gain2, bias2, bias_q, bias_v, bias_out, bias_up, bias_down = unpack(
        vectors, d, ff
    )
    first, up, downt = (blocks[0], blocks[1], blocks[2])
    factor = HD ** (-0.5)
    x = tokens.astype(F32)
    scaled1, inverse1 = norm_parts(x)
    normed1 = (scaled1 * gain1 + bias1).astype(BF16)
    mixed = jnp.einsum("rd,tdc->rtc", normed1, first[:, :, : 3 * w], preferred_element_type=F32)
    query = (mixed[:, :, :w].reshape(rows, d) + bias_q).astype(BF16).reshape(rows, heads, HD)
    key = mixed[:, :, w : 2 * w].reshape(rows, d).astype(BF16).reshape(rows, heads, HD)
    value = (mixed[:, :, 2 * w :].reshape(rows, d) + bias_v).astype(BF16).reshape(rows, heads, HD)
    images = jnp.arange(rows, dtype=jnp.int32) // patches
    allowed = images[:, None] == images[None, :]
    scores = jnp.einsum("qhd,khd->hqk", query, key, preferred_element_type=F32) * factor
    scores = jnp.where(allowed[None], scores, -1e30)
    raised = jnp.exp(scores - jnp.max(scores, axis=-1, keepdims=True))
    soft = raised / jnp.sum(raised, axis=-1, keepdims=True)
    soft_low = soft.astype(BF16)
    attended = jnp.einsum("hqk,khd->qhd", soft_low, value, preferred_element_type=F32).astype(BF16)
    flat = attended.reshape(rows, tensor, w)
    outt = first[:, :, 3 * w :]
    residual = x + jnp.einsum("rte,tde->rd", flat, outt, preferred_element_type=F32) + bias_out
    scaled2, inverse2 = norm_parts(residual)
    normed2 = (scaled2 * gain2 + bias2).astype(BF16)
    pre = jnp.einsum("rd,tdf->rtf", normed2, up, preferred_element_type=F32) + bias_up.reshape(
        tensor, c
    )
    active, slope = gelu_parts(pre)
    active = active.astype(BF16)
    second = jnp.einsum("rtf,tdf->rd", active, downt, preferred_element_type=F32)
    output = (residual + second + bias_down).astype(BF16)
    grad_active = jnp.einsum("rd,tdf->rtf", cotangent, downt, preferred_element_type=F32)
    grad_pre = (grad_active * slope).astype(BF16)
    g_down = jnp.einsum("rd,rtf->tdf", cotangent, active, preferred_element_type=F32)
    g_up = jnp.einsum("rd,rtf->tdf", normed2, grad_pre, preferred_element_type=F32)
    grad_normed2 = jnp.einsum("rtf,tdf->rd", grad_pre, up, preferred_element_type=F32)
    grad_result = cotangent.astype(F32)
    grad_residual = grad_result + norm_backward(grad_normed2, scaled2, inverse2, gain2)
    grad_branch = grad_residual.astype(BF16)
    g_outt = jnp.einsum("rd,rte->tde", grad_branch, flat, preferred_element_type=F32)
    grad_att = jnp.einsum("rd,tde->rte", grad_branch, outt, preferred_element_type=F32)
    grad_att = grad_att.astype(BF16).reshape(rows, heads, HD)
    grad_value = jnp.einsum("hqk,qhd->khd", soft_low, grad_att, preferred_element_type=F32)
    grad_soft = jnp.einsum("qhd,khd->hqk", grad_att, value, preferred_element_type=F32)
    grad_scores = (soft * (grad_soft - jnp.sum(soft * grad_soft, axis=-1, keepdims=True))).astype(
        BF16
    )
    grad_query = jnp.einsum("hqk,khd->qhd", grad_scores, key, preferred_element_type=F32) * factor
    grad_key = jnp.einsum("hqk,qhd->khd", grad_scores, query, preferred_element_type=F32) * factor
    three = [g.astype(BF16).reshape(rows, tensor, w) for g in (grad_query, grad_key, grad_value)]
    grad_mixed = jnp.concatenate(three, axis=2)
    g_qkv = jnp.einsum("rd,rtc->tdc", normed1, grad_mixed, preferred_element_type=F32)
    grad_normed1 = jnp.einsum(
        "rtc,tdc->rd", grad_mixed, first[:, :, : 3 * w], preferred_element_type=F32
    )
    grad_tokens = (grad_residual + norm_backward(grad_normed1, scaled1, inverse1, gain1)).astype(
        BF16
    )
    grads = jnp.stack(
        [
            jnp.concatenate([g_qkv, g_outt], axis=2).astype(BF16),
            g_up.astype(BF16),
            g_down.astype(BF16),
        ]
    )

    def total(values):
        return jnp.sum(values.astype(F32), axis=0).reshape(-1)

    sums = jnp.concatenate(
        [
            total(grad_normed1 * scaled1),
            total(grad_normed1),
            total(grad_normed2 * scaled2),
            total(grad_normed2),
            total(three[0]),
            total(three[2]),
            total(grad_residual),
            total(grad_pre),
            total(grad_result),
        ]
    )
    return (output, grad_tokens, grads, sums)


def make_body(dp, tensor):

    def body(
        tokens,
        cotangent,
        block_patches,
        qkv,
        out,
        up,
        down,
        vectors,
        momentum,
        target_qkv,
        target_out,
        target_up,
        target_down,
        target_vectors,
    ):
        patches = block_patches[lax.axis_index("tensor")]
        blocks = gather_blocks(pack_shards(qkv, out, up, down), dp, tensor)
        output, grad_tokens, grads, sums = local_layer(tokens, cotangent, patches, blocks, vectors)
        grads = scatter_blocks(grads, dp, tensor).astype(F32)
        sums = lax.psum(sums, BOTH)
        w = qkv.shape[2]
        rate = momentum[0]

        def average(target, online):
            return rate * target + (1.0 - rate) * online.astype(F32)

        return (
            output,
            grad_tokens,
            jnp.stack([grads[0][:, i * w : (i + 1) * w] for i in range(3)]),
            grads[0][:, 3 * w :].T,
            grads[1],
            grads[2].T,
            sums,
            average(target_qkv, qkv),
            average(target_out, out),
            average(target_up, up),
            average(target_down, down),
            average(target_vectors, vectors),
        )

    return body


def solution(mesh):
    rows, matrices = (
        P(BOTH, None),
        (P(None, "dp", "tensor"), P("tensor", "dp"), P("dp", "tensor"), P("tensor", "dp")),
    )
    return jax.shard_map(
        make_body(mesh.shape["dp"], mesh.shape["tensor"]),
        mesh=mesh,
        in_specs=(rows, rows, P("dp")) + matrices + (P(), P()) + matrices + (P(),),
        out_specs=(rows, rows) + matrices + (P(),) + matrices + (P(),),
        check_vma=False,
    )
```

profile of v0, /device:TPU:0, one launch (start us, length us, event | category | flops | bytes accessed | tf_op | source)
XLA Modules:
  0.0 541.5 jit_solution(5149204099893250085)
XLA Ops:
  9.2 1.8 pad_maximum_fusion.3
  11.1 1.2 dynamic_slice.3
  13.7 1.4 fusion.72
  17.3 100.2 %all-gather.3.cloned.1.call-done = bf16[96,96,768]{2,1,0:T(8,128)(2,1)} async-done(((bf16[3,96,768]{2,1,0:T(8,128)(2,1)}), bf16[96,96,768]{2,1,0:T(8,128)(2,1)}) %all-gather.3.cloned.1.call-update) | async-done | bytes 14155792 | tf_op jit(solution)/shard_map/all_gather | solution.py:47
  117.5 5.9 %fusion.70 = (bf16[1,4,8,96,768]{4,3,0,1,2:T(8,128)(2,1)S(1)}, bf16[1,4,8,96,768]{4,3,0,1,2:T(8,128)(2,1)S(1)}, bf16[1,4,8,96,768]{4,3,0,1,2:T(8,128)(2,1)S(1)}) fusion(bf16[3,4,8,96,768]{4,3,0,1,2:T(8,128)(2,1)} %bitcast.155), kind=kLoop, calls=%fused_computation.137 | loop fusion | bytes 28311552 | tf_op jit(solution)/shard_map/slice | solution.py:70
  123.8 2.3 slice.145
  126.1 5.8 %fusion.17 = f32[784,4,576]{2,0,1:T(8,128)} fusion(bf16[4,768,768]{2,1,0:T(8,128)(2,1)S(1)} %bitcast.158, bf16[784,768]{1,0:T(8,128)(2,1)S(1)} %copy-done.2, f32[768]{0:T(1024)S(1)} %get-tuple-element.92, f32[768]{0:T(1024)S(1)} %get-tuple-element.93, f32[784]{0:T(1024)S(1)} %add_rsqrt_fusion.1, f32[784]{0:T(1024)S(1)} %broadcast_multiply_fusion.5), kind=kOutput, calls=%fused_computation.31 | convolution fusion | flops 2778144768 | bytes 12378112 | tf_op jit(solution)/shard_map/rd,tdc->rtc/dot_general | solution.py:75
  131.9 3.0 slice.172
  134.8 6.1 %fusion.71 = (f32[784,4,192]{2,0,1:T(8,128)}, f32[784,4,192]{2,0,1:T(8,128)}) fusion(f32[784,4,576]{2,0,1:T(8,128)} %fusion.17), kind=kLoop, calls=%fused_computation.138 | loop fusion | bytes 9633792 | tf_op jit(solution)/shard_map/slice | solution.py:76
  140.9 2.5 copy.86
  143.4 2.6 copy.85
  146.0 1.6 copy.82
  147.6 2.5 copy.81
  150.1 4.6 copy.80
  154.7 19.0 %fusion.73 = (f32[12,784]{1,0:T(8,128)S(1)}, f32[12,784,784]{1,2,0:T(8,128)}) fusion(pred[784,784]{0,1:T(8,128)(4,1)S(1)} %broadcast_compare_fusion, bf16[784,12,64]{0,2,1:T(8,128)(2,1)} %bitcast.161, f32[784,12,64]{0,2,1:T(8,128)S(1)} %bitcast.152, f32[12,64]{1,0:T(8,128)S(1)} %add.137), kind=kOutput, calls=%fused_computation.140 | convolution fusion | flops 974820096 | bytes 33771520 | tf_op jit(solution)/shard_map/sub | solution.py:83
  173.7 14.8 %fusion.42 = bf16[12,64,784]{2,1,0:T(8,128)(2,1)S(1)} fusion(f32[784,12,64]{0,2,1:T(8,128)} %bitcast.175, f32[12,64]{1,0:T(8,128)S(1)} %add.133, f32[12,784,784]{1,2,0:T(8,128)} %get-tuple-element.95, f32[12,784]{1,0:T(8,128)S(1)} %get-tuple-element.94), kind=kOutput, calls=%fused_computation.77 | convolution fusion | flops 960669696 | bytes 33156864 | tf_op jit(solution)/shard_map/hqk,khd->qhd/dot_general | solution.py:86
  188.5 4.3 fusion.74
  193.3 6.2 %multiply_convert_fusion.1 = (bf16[784,4,768]{2,0,1:T(8,128)(2,1)}, f32[784,4,768]{2,0,1:T(8,128)S(1)}) fusion(f32[4,768]{1,0:T(4,128)S(1)} %slice.130, bf16[4,768,768]{2,1,0:T(8,128)(2,1)S(1)} %bitcast.173, f32[784,768]{1,0:T(8,128)S(1)} %get-tuple-element.97, f32[768]{0:T(1024)S(1)} %get-tuple-element.87, f32[768]{0:T(1024)S(1)} %get-tuple-element.88, ...), kind=kOutput, calls=%fused_computation.19 | convolution fusion | flops 3716837376 | bytes 21602432 | tf_op jit(solution)/shard_map/rd,tdf->rtf/dot_general | solution.py:92
  199.6 9.4 %convert_reduce_fusion = (f32[4,768]{1,0:T(4,128)}, bf16[784,4,768]{2,0,1:T(8,128)(2,1)S(1)}) fusion(f32[784,4,768]{2,0,1:T(8,128)S(1)} %get-tuple-element.99, f32[4,768]{1,0:T(4,128)S(1)} %slice.130, bf16[4,768,768]{2,1,0:T(8,128)(2,1)S(1)} %bitcast.170, bf16[784,768]{1,0:T(8,128)(2,1)S(1)} %copy-done.16), kind=kOutput, calls=%fused_computation.18 | convolution fusion | flops 3730682880 | bytes 20398080 | tf_op jit(solution)/shard_map/rd,tdf->rtf/dot_general | solution.py:99
  209.0 6.3 %fusion.37 = (f32[768]{0:T(1024)}, f32[784]{0:T(1024)S(1)}, f32[784]{0:T(1024)S(1)}, f32[768]{0:T(1024)}, f32[784,768,1]{1,0,2:T(8,128)}) fusion(f32[784,768]{1,0:T(8,128)S(1)} %get-tuple-element.97, f32[784]{0:T(1024)S(1)} %add_rsqrt_fusion, f32[784]{0:T(1024)S(1)} %broadcast_multiply_fusion.4, f32[768]{0:T(1024)S(1)} %get-tuple-element.88, ...), kind=kOutput, calls=%fused_computation.67 | convolution fusion | flops 3704792064 | bytes 14374144 | tf_op jit(solution)/shard_map/rtf,tdf->rd/dot_general | solution.py:103
  215.3 7.4 %convolution_convert_fusion.1 = bf16[4,768,768]{1,2,0:T(8,128)(2,1)} fusion(bf16[784,4,768]{2,0,1:T(8,128)(2,1)S(1)} %get-tuple-element.109, f32[784,768]{1,0:T(8,128)S(1)} %get-tuple-element.97, f32[768]{0:T(1024)S(1)} %get-tuple-element.87, f32[768]{0:T(1024)S(1)} %get-tuple-element.88, f32[784]{0:T(1024)S(1)} %add_rsqrt_fusion, ...), kind=kOutput, calls=%fused_computation.39 | convolution fusion | flops 3704745984 | bytes 11956352 | tf_op jit(solution)/shard_map/rd,rtf->tdf/dot_general | solution.py:102
  222.7 2.6 copy.103
  225.3 3.3 fusion.69
  228.7 2.4 fusion.48
  231.1 1.4 fusion.55
  232.5 1.3 convert_element_type.135
  233.8 15.6 %convert_reduce_fusion.3 = (f32[12,64]{1,0:T(8,128)}, bf16[12,64,784]{2,1,0:T(8,128)(2,1)}) fusion(bf16[784,12,64]{0,2,1:T(8,128)(2,1)} %bitcast.179, f32[12,784,784]{1,2,0:T(8,128)} %get-tuple-element.95, f32[12,784]{1,0:T(8,128)S(1)} %get-tuple-element.94), kind=kOutput, calls=%fused_computation.46 | convolution fusion | flops 960668928 | bytes 31952640 | tf_op jit(solution)/shard_map/hqk,qhd->khd/dot_general | solution.py:110
  249.4 25.2 %multiply_reduce_fusion = (f32[12,784]{1,0:T(8,128)S(1)}, f32[12,784,784]{1,2,0:T(8,128)}) fusion(f32[12,784,784]{1,2,0:T(8,128)} %get-tuple-element.95, f32[12,784]{1,0:T(8,128)S(1)} %get-tuple-element.94, bf16[784,12,64]{0,2,1:T(8,128)(2,1)} %bitcast.180, f32[784,12,64]{0,2,1:T(8,128)S(1)} %bitcast.176, f32[12,64]{1,0:T(8,128)S(1)} %add.133), kind=kOutput, calls=%fused_computation.2 | convolution fusion | flops 967434048 | bytes 62697984 | tf_op jit(solution)/shard_map/qhd,khd->hqk/dot_general | solution.py:111
  274.6 27.9 %multiply_convert_fusion = bf16[12,784,784]{1,2,0:T(8,128)(2,1)} fusion(f32[12,784,784]{1,2,0:T(8,128)} %get-tuple-element.102, f32[12,784]{1,0:T(8,128)S(1)} %get-tuple-element.101, f32[12,784,784]{1,2,0:T(8,128)} %get-tuple-element.95, f32[12,784]{1,0:T(8,128)S(1)} %get-tuple-element.94), kind=kLoop, calls=%fused_computation.1 | loop fusion | flops 29503488 | bytes 73833984 | tf_op jit(solution)/shard_map/convert_element_type | solution.py:112
  302.5 10.1 %multiply_convert_fusion.2 = bf16[12,64,784]{2,1,0:T(8,128)(2,1)} fusion(bf16[12,784,784]{1,2,0:T(8,128)(2,1)} %multiply_convert_fusion, f32[784,12,64]{0,2,1:T(8,128)S(1)} %bitcast.153, f32[12,64]{1,0:T(8,128)S(1)} %copy-done.26), kind=kOutput, calls=%fused_computation.48 | convolution fusion | flops 946520064 | bytes 18367488 | tf_op jit(solution)/shard_map/hqk,qhd->khd/dot_general | solution.py:116
  312.7 10.8 %convert_reduce_fusion.4 = (f32[12,64]{1,0:T(8,128)}, bf16[12,64,784]{2,1,0:T(8,128)(2,1)}) fusion(bf16[784,12,64]{0,2,1:T(8,128)(2,1)S(1)} %bitcast.162, bf16[12,784,784]{1,2,0:T(8,128)(2,1)} %multiply_convert_fusion), kind=kOutput, calls=%fused_computation.47 | convolution fusion | flops 946519296 | bytes 17163264 | tf_op jit(solution)/shard_map/hqk,khd->qhd/dot_general | solution.py:115
  323.5 9.2 %convolution_convert_fusion = bf16[4,768,768]{1,2,0:T(8,128)(2,1)} fusion(bf16[784,4,768]{2,0,1:T(8,128)(2,1)} %get-tuple-element.98, bf16[784,768]{1,0:T(8,128)(2,1)S(1)} %copy-done.17), kind=kOutput, calls=%fused_computation.38 | convolution fusion | flops 3701735424 | bytes 10739712 | tf_op jit(solution)/shard_map/rd,rtf->tdf/dot_general | solution.py:101
  332.7 1.6 copy.101
  334.3 2.6 copy.92
  337.0 1.7 copy.91
  338.6 2.7 copy.90
  341.4 8.5 %convert_bitcast_fusion = bf16[4,768,576]{1,2,0:T(8,128)(2,1)} fusion(bf16[784,4,192]{2,0,1:T(8,128)(2,1)S(1)} %copy-done.14, bf16[784,4,192]{2,0,1:T(8,128)(2,1)} %copy.91, bf16[784,4,192]{2,0,1:T(8,128)(2,1)} %copy.90, bf16[784,768]{1,0:T(8,128)(2,1)S(1)} %copy-done.4, f32[768]{0:T(1024)S(1)} %copy-done.40, f32[768]{0:T(1024)S(1)} %copy-done.32, ...), kind=kOutput, calls=%fused_computation.30 | convolution fusion | flops 2790752256 | bytes 8368256 | tf_op jit(solution)/shard_map/rd,rtc->tdc/dot_general | solution.py:119
  350.0 6.1 %copy.93 = bf16[4,768,576]{2,1,0:T(8,128)(2,1)} copy(bf16[4,768,576]{1,2,0:T(8,128)(2,1)} %convert_bitcast_fusion) | data formatting | bytes 7077888 | tf_op jit(solution)/shard_map/rd,rtc->tdc/transpose | solution.py:119
  356.0 7.7 %maximum_bitcast_fusion = bf16[8,4,3,96,768]{4,3,0,1,2:T(8,128)(2,1)S(1)} fusion(bf16[1,4,8,96,768]{4,3,2,1,0:T(8,128)(2,1)} %bitcast.166, bf16[1,4,8,96,768]{4,3,2,1,0:T(8,128)(2,1)} %bitcast.165, bf16[1,4,8,96,192]{4,3,2,1,0:T(8,128)(2,1)S(1)} %bitcast.164, bf16[1,4,8,96,576]{4,3,2,1,0:T(8,128)(2,1)} %bitcast.154), kind=kLoop, calls=%fused_computation.11 | loop fusion | flops 56623104 | bytes 28311552 | tf_op jit(solution)/shard_map/transpose | solution.py:56
  363.7 6.0 %copy.95 = bf16[8,4,3,96,768]{4,3,2,1,0:T(8,128)(2,1)} copy(bf16[8,4,3,96,768]{4,3,0,1,2:T(8,128)(2,1)S(1)} %maximum_bitcast_fusion) | data formatting | bytes 28311552 | tf_op jit(solution)/shard_map/transpose | solution.py:56
  370.5 1.6 multiply_add_fusion.3
  372.9 1.7 multiply_add_fusion.1
  374.6 1.7 multiply_add_fusion
  379.3 8.7 %fusion.34 = (f32[768]{0:T(1024)S(1)}, f32[784]{0:T(1024)S(1)}, f32[784]{0:T(1024)S(1)}, f32[768]{0:T(1024)S(1)}, f32[784,768,1]{1,0,2:T(8,128)}) fusion(bf16[784,768]{1,0:T(8,128)(2,1)S(1)} %copy-done.4, f32[784]{0:T(1024)} %copy-done.33, f32[784]{0:T(1024)S(1)} %copy-done.28, f32[768]{0:T(1024)S(1)} %copy-done.32, bf16[4,768,768]{2,1,0:T(8,128)(2,1)} %bitcast.160, ...), kind=kOutput, calls=%fused_computation.59 | convolution fusion | flops 2791388160 | bytes 11983040 | tf_op jit(solution)/shard_map/rtc,tdc->rd/dot_general | solution.py:120
  388.1 39.2 %psum.7 = f32[9216]{0:T(1024)} all-reduce(f32[9216]{0:T(1024)S(1)} %constant_dynamic-update-slice_fusion), channel_id=1, replica_groups=mesh['dp'=8,'tensor'=4] {'dp','tensor'}, use_global_device_ids=true, to_apply=%region_21.22 | all-reduce | flops 9216 | bytes 73728 | tf_op jit(solution)/shard_map/psum | solution.py:175
  427.4 3.8 fusion.33
  431.2 8.8 %fusion.39 = bf16[784,768]{1,0:T(8,128)(2,1)} fusion(f32[784,768]{1,0:T(8,128)S(1)} %copy-done.9, bf16[784,4,768]{2,0,1:T(8,128)(2,1)} %get-tuple-element.98, bf16[4,768,768]{2,1,0:T(8,128)(2,1)} %bitcast.167, f32[768]{0:T(1024)S(1)} %copy-done.38), kind=kOutput, calls=%fused_computation.70 | convolution fusion | flops 3701182464 | bytes 13151232 | tf_op jit(solution)/shard_map/rtf,tdf->rd/dot_general | solution.py:97
  440.0 90.7 %reduce-scatter.2.cloned.1.call-done = bf16[1,3,96,768]{3,2,1,0:T(8,128)(2,1)} async-done(((bf16[32,3,96,768]{3,2,1,0:T(8,128)(2,1)}), bf16[1,3,96,768]{3,2,1,0:T(8,128)(2,1)}) %reduce-scatter.2.cloned.1.call-update) | async-done | bytes 442384 | tf_op jit(solution)/shard_map/reduce_scatter | solution.py:58
  (144 shorter events, 13.2 us)
Async XLA Ops:
  7.2 8.8 %copy-start.2 = (bf16[784,768]{1,0:T(8,128)(2,1)S(1)}, bf16[784,768]{1,0:T(8,128)(2,1)}, u32[]{:S(2)}) copy-start(bf16[784,768]{1,0:T(8,128)(2,1)} %param.14) | copy-start | bytes 3612676
  7.2 110.3 %all-gather.3.cloned.1.call-start = ((), (), s32[]{:S(2)}) async-start(), calls=%async_computation.2 | async-start | bytes 14598144 | tf_op jit(solution)/shard_map/all_gather | solution.py:47
  11.0 519.7 %reduce-scatter.2.cloned.1.call-start = ((), (), s32[]{:S(2)}) async-start(), calls=%async_computation.1 | async-start | bytes 14598144 | tf_op jit(solution)/shard_map/reduce_scatter | solution.py:58
  15.1 111.0 %copy-start.31 = (f32[768]{0:T(1024)}, f32[768]{0:T(1024)S(1)}, u32[]{:S(2)}) copy-start(f32[768]{0:T(1024)S(1)} %get-tuple-element.93) | copy-start | bytes 9220
  15.1 111.0 %copy-start.39 = (f32[768]{0:T(1024)}, f32[768]{0:T(1024)S(1)}, u32[]{:S(2)}) copy-start(f32[768]{0:T(1024)S(1)} %get-tuple-element.92) | copy-start | bytes 9220
  15.2 139.5 %copy-start.25 = (f32[12,64]{1,0:T(8,128)}, f32[12,64]{1,0:T(8,128)S(1)}, u32[]{:S(2)}) copy-start(f32[12,64]{1,0:T(8,128)S(1)} %add.137) | copy-start | bytes 9220
  16.3 109.8 %copy-start.27 = (f32[784]{0:T(1024)}, f32[784]{0:T(1024)S(1)}, u32[]{:S(2)}) copy-start(f32[784]{0:T(1024)S(1)} %broadcast_multiply_fusion.5) | copy-start | bytes 9412
  16.8 109.2 %copy-start.33 = (f32[784]{0:T(1024)}, f32[784]{0:T(1024)S(1)}, u32[]{:S(2)}) copy-start(f32[784]{0:T(1024)S(1)} %add_rsqrt_fusion.1) | copy-start | bytes 9412
  123.7 8.1 %copy-start.10 = (bf16[1,4,8,96,768]{4,3,2,1,0:T(8,128)(2,1)}, bf16[1,4,8,96,768]{4,3,2,1,0:T(8,128)(2,1)S(1)}, u32[]{:S(2)}) copy-start(bf16[1,4,8,96,768]{4,3,2,1,0:T(8,128)(2,1)S(1)} %copy.78) | copy-start | bytes 14155780
  150.1 4.6 copy-start
  173.6 14.8 %copy-start.3 = (bf16[784,768]{1,0:T(8,128)(2,1)S(1)}, bf16[784,768]{1,0:T(8,128)(2,1)}, u32[]{:S(2)}) copy-start(bf16[784,768]{1,0:T(8,128)(2,1)} %param.14) | copy-start | bytes 3612676
  188.5 4.3 copy-start.43
  188.5 4.8 slice-start.2
  188.5 4.8 slice-start.3
  188.5 11.1 %slice-start = ((s8[4718592]{0:T(1024)(128)(4,1)}), s8[4194304]{0:T(1024)(128)(4,1)S(1)}, s32[]{:S(2)}) async-start(s8[4718592]{0:T(1024)(128)(4,1)} %bitcast.168), calls=%async_computation.3 | async-start | bytes 8388608
  192.8 22.5 %copy-start.7 = (f32[784,768]{1,0:T(8,128)}, f32[784,768]{1,0:T(8,128)S(1)}, u32[]{:S(2)}) copy-start(f32[784,768]{1,0:T(8,128)S(1)} %get-tuple-element.97) | copy-start | bytes 7225348
  193.3 6.3 %slice-start.1 = ((s8[4718592]{0:T(1024)(128)(4,1)}), s8[524288]{0:T(1024)(128)(4,1)S(1)}, s32[]{:S(2)}) async-start(s8[4718592]{0:T(1024)(128)(4,1)} %bitcast.168), calls=%async_computation.4 | async-start | bytes 1048576
  193.3 6.2 %copy-start.16 = (bf16[784,768]{1,0:T(8,128)(2,1)S(1)}, bf16[784,768]{1,0:T(8,128)(2,1)}, u32[]{:S(2)}) copy-start(bf16[784,768]{1,0:T(8,128)(2,1)} %param.15) | copy-start | bytes 3612676
  222.7 2.6 copy-start.8
  225.3 3.3 copy-start.44
  233.8 15.6 %copy-start.13 = (f32[784,4,192]{0,2,1:T(8,128)S(1)}, f32[784,4,192]{0,2,1:T(8,128)}, u32[]{:S(2)}) copy-start(f32[784,4,192]{0,2,1:T(8,128)} %copy.80) | copy-start | bytes 7225348
  274.6 27.9 %copy-start.1 = (f32[784,4,192]{0,2,1:T(8,128)S(1)}, f32[784,4,192]{0,2,1:T(8,128)}, u32[]{:S(2)}) copy-start(f32[784,4,192]{0,2,1:T(8,128)} %copy-done) | copy-start | bytes 7225348
  274.6 27.9 %copy-start.26 = (f32[12,64]{1,0:T(8,128)S(1)}, f32[12,64]{1,0:T(8,128)}, u32[]{:S(2)}) copy-start(f32[12,64]{1,0:T(8,128)} %copy-done.25) | copy-start | bytes 9220
  302.5 10.1 %copy-start.11 = (bf16[784,4,192]{0,2,1:T(8,128)(2,1)S(1)}, bf16[784,4,192]{0,2,1:T(8,128)(2,1)}, u32[]{:S(2)}) copy-start(bf16[784,4,192]{0,2,1:T(8,128)(2,1)} %copy.82) | copy-start | bytes 3612676
  312.7 10.8 %copy-start.17 = (bf16[784,768]{1,0:T(8,128)(2,1)S(1)}, bf16[784,768]{1,0:T(8,128)(2,1)}, u32[]{:S(2)}) copy-start(bf16[784,768]{1,0:T(8,128)(2,1)} %param.15) | copy-start | bytes 3612676
  323.5 9.2 %copy-start.18 = (bf16[4,768,192]{1,2,0:T(8,128)(2,1)S(1)}, bf16[4,768,192]{1,2,0:T(8,128)(2,1)}, u32[]{:S(2)}) copy-start(bf16[4,768,192]{1,2,0:T(8,128)(2,1)} %fusion.48) | copy-start | bytes 3538948
  332.7 4.2 copy-start.5
  336.9 4.5 copy-start.4
  336.9 4.5 copy-start.28
  336.9 4.5 copy-start.32
  336.9 4.4 copy-start.34
  336.9 4.4 copy-start.40
  338.6 2.8 copy-start.14
  350.0 6.1 %copy-start.12 = (bf16[4,768,192]{2,1,0:T(8,128)(2,1)S(1)}, bf16[4,768,192]{2,1,0:T(8,128)(2,1)}, u32[]{:S(2)}) copy-start(bf16[4,768,192]{2,1,0:T(8,128)(2,1)} %copy.101) | copy-start | bytes 3538948
  369.7 2.5 copy-start.23
  369.7 3.2 copy-start.20
  369.7 5.0 copy-start.21
  369.7 9.6 %copy-start.15 = (bf16[784,4,192]{2,0,1:T(8,128)(2,1)S(1)}, bf16[784,4,192]{2,0,1:T(8,128)(2,1)}, u32[]{:S(2)}) copy-start(bf16[784,4,192]{2,0,1:T(8,128)(2,1)} %copy.92) | copy-start | bytes 3612676
  370.5 5.9 %copy-start.24 = (f32[9216]{0:T(1024)S(1)}, f32[9216]{0:T(1024)}, u32[]{:S(2)}) copy-start(f32[9216]{0:T(1024)} %param.21) | copy-start | bytes 110596
  370.5 5.8 %copy-start.29 = (f32[9216]{0:T(1024)S(1)}, f32[9216]{0:T(1024)}, u32[]{:S(2)}) copy-start(f32[9216]{0:T(1024)} %param.27) | copy-start | bytes 110596
  379.3 8.7 %copy-start.30 = (f32[9216]{0:T(1024)S(1)}, f32[9216]{0:T(1024)}, u32[]{:S(2)}) copy-start(f32[9216]{0:T(1024)} %custom-call) | copy-start | bytes 110596
  379.3 8.8 %copy-start.42 = (f32[768]{0:T(1024)S(1)}, f32[768]{0:T(1024)}, u32[]{:S(2)}) copy-start(f32[768]{0:T(1024)} %get-tuple-element.60) | copy-start | bytes 9220
  379.3 8.8 %copy-start.41 = (f32[768]{0:T(1024)S(1)}, f32[768]{0:T(1024)}, u32[]{:S(2)}) copy-start(f32[768]{0:T(1024)} %get-tuple-element.66) | copy-start | bytes 9220
  379.3 8.8 %copy-start.37 = (f32[768]{0:T(1024)S(1)}, f32[768]{0:T(1024)}, u32[]{:S(2)}) copy-start(f32[768]{0:T(1024)} %get-tuple-element.68) | copy-start | bytes 9220
  379.3 8.8 %copy-start.36 = (f32[768]{0:T(1024)S(1)}, f32[768]{0:T(1024)}, u32[]{:S(2)}) copy-start(f32[768]{0:T(1024)} %get-tuple-element.75) | copy-start | bytes 9220
  379.3 48.1 %copy-start.35 = (f32[784]{0:T(1024)S(1)}, f32[784]{0:T(1024)}, u32[]{:S(2)}) copy-start(f32[784]{0:T(1024)} %copy-done.33) | copy-start | bytes 9412
  427.4 3.8 copy-start.9
  427.4 3.8 copy-start.38
  (3 other events, 7.3 us)
Sparse Core Ops, SparseCore 0:
  11.5 105.9 all-gather.2
  369.8 160.8 reduce-scatter.1
where the time goes:
time: 552 us; the launch traced here: 542 us
  waiting for transfers between devices  191 us (35%)
  matrix products  174 us (32%)
  local copies, waits for them, and re-layouts  64.2 us (12%)
  other arithmetic  56.6 us (10%)
  blocking collectives  39.2 us (7%)
  between operations  16.5 us (3%)
    all_gather x1, waiting for transfers between devices, gather_blocks(): every = lax.all_gather(shards, BOTH, axis=0)  100 us
    reduce_scatter x1, waiting for transfers between devices, scatter_blocks(): return lax.psum_scatter(pieces, BOTH, scatter_dimension=0, tiled=True)[0]  90.7 us
    psum x1, blocking collectives, body(): sums = lax.psum(sums, BOTH)  39.2 us
    convert_element_type x1, other arithmetic, local_layer(): (soft * (grad_soft - jnp.sum(soft * grad_soft, axis=-1, keepdims=True)))....  27.9 us
    dot_general x1, matrix products, local_layer(): jnp.einsum('qhd,khd->hqk', grad_att, value, preferred_element_type=F32)  25.2 us
    sub x1, matrix products, local_layer(): raised = jnp.exp(scores - jnp.max(scores, axis=-1, keepdims=True))  19 us
    dot_general x1, matrix products, local_layer(): jnp.einsum('hqk,qhd->khd', soft_low, grad_att, preferred_element_type=F32)  15.6 us
    dot_general x1, matrix products, local_layer(): jnp.einsum('hqk,khd->qhd', soft_low, value, preferred_element_type=F32)  14.8 us
  transfers between devices with their start and end apart: 2, of which 2 were waited for; matrix products, arithmetic and copies ran while one was open for 7% of the time, Pallas kernels for 0%

commit v1 on v0

--- a/solution.py
+++ b/solution.py
@@ -172,7 +172,7 @@
         blocks = gather_blocks(pack_shards(qkv, out, up, down), dp, tensor)
         output, grad_tokens, grads, sums = local_layer(tokens, cotangent, patches, blocks, vectors)
         grads = scatter_blocks(grads, dp, tensor).astype(F32)
-        sums = lax.psum(sums, BOTH)
+        sums = jnp.sum(lax.all_gather(sums, BOTH), axis=0)
         w = qkv.shape[2]
         rate = momentum[0]
 

time: 552 us -> 581 us (1.053)
  waiting for transfers between devices: 191 us -> 275 us
  blocking collectives: 39.2 us -> 0 us
    reduce_scatter x1, waiting for transfers between devices: 90.7 us -> 166 us  [scatter_blocks(): return lax.psum_scatter(pieces, BOTH, scatter_dimension=0, tiled=True)[0]]
    psum x1 -> x0, blocking collectives: 39.2 us -> none  [body(): sums = lax.psum(sums, BOTH)]
    all_gather x0 -> x1, waiting for transfers between devices: none -> 9.83 us  [body(): sums = jnp.sum(lax.all_gather(sums, BOTH), axis=0)]
  transfers between devices with their start and end apart: 2 -> 3, of which waited for: 2 -> 3; matrix products, arithmetic and copies ran while one was open for 7% -> 9% of each run, Pallas kernels for 0% -> 0%
where the time goes in v1:
time: 581 us; the launch traced here: 574 us
  waiting for transfers between devices  275 us (47%)
  matrix products  170 us (29%)
  local copies, waits for them, and re-layouts  61.2 us (11%)
  other arithmetic  51.4 us (9%)
  between operations  16.1 us (3%)
    reduce_scatter x1, waiting for transfers between devices, scatter_blocks(): return lax.psum_scatter(pieces, BOTH, scatter_dimension=0, tiled=True)[0]  166 us
    all_gather x1, waiting for transfers between devices, gather_blocks(): every = lax.all_gather(shards, BOTH, axis=0)  99.3 us
    convert_element_type x1, other arithmetic, local_layer(): (soft * (grad_soft - jnp.sum(soft * grad_soft, axis=-1, keepdims=True)))....  27.9 us
    dot_general x1, matrix products, local_layer(): jnp.einsum('qhd,khd->hqk', grad_att, value, preferred_element_type=F32)  25.6 us
    sub x1, matrix products, local_layer(): raised = jnp.exp(scores - jnp.max(scores, axis=-1, keepdims=True))  18.8 us
    dot_general x1, matrix products, local_layer(): jnp.einsum('hqk,qhd->khd', soft_low, grad_att, preferred_element_type=F32)  15 us
    dot_general x1, matrix products, local_layer(): jnp.einsum('hqk,khd->qhd', soft_low, value, preferred_element_type=F32)  14.8 us
  transfers between devices with their start and end apart: 3, of which 3 were waited for; matrix products, arithmetic and copies ran while one was open for 9% of the time, Pallas kernels for 0%

profile of v1, /device:TPU:0, one launch (start us, length us, event | category | flops | bytes accessed | tf_op | source)
XLA Modules:
  0.0 573.8 jit_solution(10394894747638937004)
XLA Ops:
  7.2 1.0 copy.97
  9.2 1.8 pad_maximum_fusion.3
  11.1 1.2 dynamic_slice.3
  13.7 1.4 fusion.72
  16.9 1.3 broadcast_compare_fusion
  18.2 99.3 %all-gather.5.cloned.1.call-done = bf16[96,96,768]{2,1,0:T(8,128)(2,1)} async-done(((bf16[3,96,768]{2,1,0:T(8,128)(2,1)}), bf16[96,96,768]{2,1,0:T(8,128)(2,1)}) %all-gather.5.cloned.1.call-update) | async-done | bytes 14155792 | tf_op jit(solution)/shard_map/all_gather | solution.py:47
  117.5 5.9 %fusion.70 = (bf16[1,4,8,96,768]{4,3,0,1,2:T(8,128)(2,1)S(1)}, bf16[1,4,8,96,768]{4,3,0,1,2:T(8,128)(2,1)S(1)}, bf16[1,4,8,96,768]{4,3,0,1,2:T(8,128)(2,1)S(1)}) fusion(bf16[3,4,8,96,768]{4,3,0,1,2:T(8,128)(2,1)} %bitcast.155), kind=kLoop, calls=%fused_computation.137 | loop fusion | bytes 28311552 | tf_op jit(solution)/shard_map/slice | solution.py:70
  124.5 5.8 %fusion.17 = f32[784,4,576]{2,0,1:T(8,128)} fusion(bf16[4,768,768]{2,1,0:T(8,128)(2,1)S(1)} %bitcast.158, bf16[784,768]{1,0:T(8,128)(2,1)S(1)} %copy-done.3, f32[768]{0:T(1024)S(1)} %get-tuple-element.104, f32[768]{0:T(1024)S(1)} %get-tuple-element.105, f32[784]{0:T(1024)S(1)} %add_rsqrt_fusion.1, f32[784]{0:T(1024)S(1)} %broadcast_multiply_fusion.5), kind=kOutput, calls=%fused_computation.31 | convolution fusion | flops 2778144768 | bytes 12378112 | tf_op jit(solution)/shard_map/rd,tdc->rtc/dot_general | solution.py:75
  130.3 3.0 slice.172
  133.3 6.0 %fusion.71 = (f32[784,4,192]{2,0,1:T(8,128)}, f32[784,4,192]{2,0,1:T(8,128)}) fusion(f32[784,4,576]{2,0,1:T(8,128)} %fusion.17), kind=kLoop, calls=%fused_computation.138 | loop fusion | bytes 9633792 | tf_op jit(solution)/shard_map/slice | solution.py:76
  139.3 2.6 copy.106
  141.9 2.6 copy.105
  144.5 1.5 copy.123
  146.0 1.6 copy.102
  147.6 2.5 copy.101
  150.1 4.6 copy.100
  154.6 18.8 %fusion.73 = (f32[12,784]{1,0:T(8,128)S(1)}, f32[12,784,784]{1,2,0:T(8,128)}) fusion(pred[784,784]{0,1:T(8,128)(4,1)S(1)} %copy-done.20, bf16[784,12,64]{0,2,1:T(8,128)(2,1)} %bitcast.161, f32[784,12,64]{0,2,1:T(8,128)S(1)} %bitcast.152, f32[12,64]{1,0:T(8,128)S(1)} %add.135), kind=kOutput, calls=%fused_computation.140 | convolution fusion | flops 974820096 | bytes 33771520 | tf_op jit(solution)/shard_map/sub | solution.py:83
  173.5 14.8 %fusion.42 = bf16[12,64,784]{2,1,0:T(8,128)(2,1)S(1)} fusion(f32[784,12,64]{0,2,1:T(8,128)} %bitcast.175, f32[12,64]{1,0:T(8,128)S(1)} %add.131, f32[12,784,784]{1,2,0:T(8,128)} %get-tuple-element.107, f32[12,784]{1,0:T(8,128)S(1)} %get-tuple-element.106), kind=kOutput, calls=%fused_computation.77 | convolution fusion | flops 960669696 | bytes 33156864 | tf_op jit(solution)/shard_map/hqk,khd->qhd/dot_general | solution.py:86
  188.3 3.9 fusion.74
  192.8 6.5 %multiply_convert_fusion.1 = (bf16[784,4,768]{2,0,1:T(8,128)(2,1)}, f32[784,4,768]{2,0,1:T(8,128)S(1)}) fusion(f32[4,768]{1,0:T(4,128)S(1)} %slice.130, bf16[4,768,768]{2,1,0:T(8,128)(2,1)S(1)} %bitcast.173, f32[784,768]{1,0:T(8,128)S(1)} %get-tuple-element.109, f32[768]{0:T(1024)S(1)} %get-tuple-element.99, f32[768]{0:T(1024)S(1)} %get-tuple-element.100, ...), kind=kOutput, calls=%fused_computation.19 | convolution fusion | flops 3716837376 | bytes 21602432 | tf_op jit(solution)/shard_map/rd,tdf->rtf/dot_general | solution.py:92
  199.3 9.4 %convert_reduce_fusion = (f32[4,768]{1,0:T(4,128)}, bf16[784,4,768]{2,0,1:T(8,128)(2,1)S(1)}) fusion(f32[784,4,768]{2,0,1:T(8,128)S(1)} %get-tuple-element.111, f32[4,768]{1,0:T(4,128)S(1)} %slice.130, bf16[4,768,768]{2,1,0:T(8,128)(2,1)S(1)} %bitcast.170, bf16[784,768]{1,0:T(8,128)(2,1)S(1)} %copy-done.17), kind=kOutput, calls=%fused_computation.18 | convolution fusion | flops 3730682880 | bytes 20398080 | tf_op jit(solution)/shard_map/rd,tdf->rtf/dot_general | solution.py:99
  208.7 4.9 fusion.37
  213.6 1.9 fusion.69
  215.5 2.4 fusion.48
  217.9 1.4 fusion.55
  219.3 1.3 convert_element_type.135
  220.6 15.0 %convert_reduce_fusion.3 = (f32[12,64]{1,0:T(8,128)S(1)}, bf16[12,64,784]{2,1,0:T(8,128)(2,1)}) fusion(bf16[784,12,64]{0,2,1:T(8,128)(2,1)} %bitcast.179, f32[12,784,784]{1,2,0:T(8,128)} %get-tuple-element.107, f32[12,784]{1,0:T(8,128)S(1)} %get-tuple-element.106), kind=kOutput, calls=%fused_computation.46 | convolution fusion | flops 960668928 | bytes 31952640 | tf_op jit(solution)/shard_map/hqk,qhd->khd/dot_general | solution.py:110
  235.6 25.6 %multiply_reduce_fusion = (f32[12,784]{1,0:T(8,128)S(1)}, f32[12,784,784]{1,2,0:T(8,128)}) fusion(f32[12,784,784]{1,2,0:T(8,128)} %get-tuple-element.107, f32[12,784]{1,0:T(8,128)S(1)} %get-tuple-element.106, bf16[784,12,64]{0,2,1:T(8,128)(2,1)} %bitcast.180, f32[784,12,64]{0,2,1:T(8,128)S(1)} %bitcast.176, f32[12,64]{1,0:T(8,128)S(1)} %add.131), kind=kOutput, calls=%fused_computation.2 | convolution fusion | flops 967434048 | bytes 62697984 | tf_op jit(solution)/shard_map/qhd,khd->hqk/dot_general | solution.py:111
  261.3 27.9 %multiply_convert_fusion = bf16[12,784,784]{1,2,0:T(8,128)(2,1)} fusion(f32[12,784,784]{1,2,0:T(8,128)} %get-tuple-element.114, f32[12,784]{1,0:T(8,128)S(1)} %get-tuple-element.113, f32[12,784,784]{1,2,0:T(8,128)} %get-tuple-element.107, f32[12,784]{1,0:T(8,128)S(1)} %get-tuple-element.106), kind=kLoop, calls=%fused_computation.1 | loop fusion | flops 29503488 | bytes 73833984 | tf_op jit(solution)/shard_map/convert_element_type | solution.py:112
  289.1 10.0 %multiply_convert_fusion.2 = bf16[12,64,784]{2,1,0:T(8,128)(2,1)} fusion(bf16[12,784,784]{1,2,0:T(8,128)(2,1)} %multiply_convert_fusion, f32[784,12,64]{0,2,1:T(8,128)S(1)} %bitcast.153, f32[12,64]{1,0:T(8,128)S(1)} %copy-done.30), kind=kOutput, calls=%fused_computation.48 | convolution fusion | flops 946520064 | bytes 18367488 | tf_op jit(solution)/shard_map/hqk,qhd->khd/dot_general | solution.py:116
  299.1 10.1 %convert_reduce_fusion.4 = (f32[12,64]{1,0:T(8,128)S(1)}, bf16[12,64,784]{2,1,0:T(8,128)(2,1)}) fusion(bf16[784,12,64]{0,2,1:T(8,128)(2,1)S(1)} %bitcast.162, bf16[12,784,784]{1,2,0:T(8,128)(2,1)} %multiply_convert_fusion), kind=kOutput, calls=%fused_computation.47 | convolution fusion | flops 946519296 | bytes 17163264 | tf_op jit(solution)/shard_map/hqk,khd->qhd/dot_general | solution.py:115
  309.2 2.7 copy.112
  311.9 1.7 copy.111
  313.6 2.7 copy.110
  316.4 8.4 %fusion.34 = (f32[768]{0:T(1024)S(1)}, f32[784]{0:T(1024)S(1)}, f32[784]{0:T(1024)S(1)}, f32[768]{0:T(1024)S(1)}, f32[784,768,1]{1,0,2:T(8,128)}) fusion(bf16[784,768]{1,0:T(8,128)(2,1)S(1)} %copy-done.5, f32[784]{0:T(1024)S(1)} %copy-done.44, f32[784]{0:T(1024)S(1)} %copy-done.33, f32[768]{0:T(1024)S(1)} %copy-done.40, bf16[4,768,768]{2,1,0:T(8,128)(2,1)} %bitcast.160, ...), kind=kOutput, calls=%fused_computation.59 | convolution fusion | flops 2791388160 | bytes 11982080 | tf_op jit(solution)/shard_map/rtc,tdc->rd/dot_general | solution.py:120
  324.8 6.8 %convert_bitcast_fusion = bf16[4,768,576]{1,2,0:T(8,128)(2,1)} fusion(bf16[784,4,192]{2,0,1:T(8,128)(2,1)S(1)} %copy-done.14, bf16[784,4,192]{2,0,1:T(8,128)(2,1)S(1)} %copy-done.15, bf16[784,4,192]{2,0,1:T(8,128)(2,1)S(1)} %copy-done.16, bf16[784,768]{1,0:T(8,128)(2,1)S(1)} %copy-done.5, f32[768]{0:T(1024)S(1)} %copy-done.54, f32[768]{0:T(1024)S(1)} %copy-done.40, ...), kind=kOutput, calls=%fused_computation.30 | convolution fusion | flops 2790752256 | bytes 8368256 | tf_op jit(solution)/shard_map/rd,rtc->tdc/dot_general | solution.py:119
  331.6 9.1 %convolution_convert_fusion = bf16[4,768,768]{1,2,0:T(8,128)(2,1)} fusion(bf16[784,4,768]{2,0,1:T(8,128)(2,1)} %get-tuple-element.110, bf16[784,768]{1,0:T(8,128)(2,1)S(1)} %copy-done.18), kind=kOutput, calls=%fused_computation.38 | convolution fusion | flops 3701735424 | bytes 10739712 | tf_op jit(solution)/shard_map/rd,rtf->tdf/dot_general | solution.py:101
  340.8 1.7 copy.121
  343.5 5.9 %copy.113 = bf16[4,768,576]{2,1,0:T(8,128)(2,1)} copy(bf16[4,768,576]{1,2,0:T(8,128)(2,1)} %convert_bitcast_fusion) | data formatting | bytes 7077888 | tf_op jit(solution)/shard_map/rd,rtc->tdc/transpose | solution.py:119
  349.4 8.5 %convolution_convert_fusion.1 = bf16[4,768,768]{1,2,0:T(8,128)(2,1)S(1)} fusion(bf16[784,4,768]{2,0,1:T(8,128)(2,1)} %copy-done.57, f32[784,768]{1,0:T(8,128)} %copy-done.9, f32[768]{0:T(1024)S(1)} %copy-done.52, f32[768]{0:T(1024)S(1)} %copy-done.42, f32[784]{0:T(1024)S(1)} %copy-done.46, f32[784]{0:T(1024)S(1)} %copy-done.35), kind=kOutput, calls=%fused_computation.39 | convolution fusion | flops 3704745984 | bytes 11956352 | tf_op jit(solution)/shard_map/rd,rtf->tdf/dot_general | solution.py:102
  357.9 5.8 %maximum_bitcast_fusion = bf16[8,4,3,96,768]{4,3,0,1,2:T(8,128)(2,1)S(1)} fusion(bf16[1,4,8,96,768]{4,3,2,1,0:T(8,128)(2,1)} %bitcast.165, bf16[1,4,8,96,768]{4,3,2,1,0:T(8,128)(2,1)S(1)} %bitcast.166, bf16[1,4,8,96,192]{4,3,2,1,0:T(8,128)(2,1)S(1)} %bitcast.164, bf16[1,4,8,96,576]{4,3,2,1,0:T(8,128)(2,1)S(1)} %bitcast.154), kind=kLoop, calls=%fused_computation.11 | loop fusion | flops 56623104 | bytes 28311552 | tf_op jit(solution)/shard_map/transpose | solution.py:56
  363.8 5.6 copy.115
  373.9 3.3 fusion.33
  377.2 8.8 %fusion.39 = bf16[784,768]{1,0:T(8,128)(2,1)} fusion(f32[784,768]{1,0:T(8,128)S(1)} %copy-done.10, bf16[784,4,768]{2,0,1:T(8,128)(2,1)} %get-tuple-element.110, bf16[4,768,768]{2,1,0:T(8,128)(2,1)} %bitcast.167, f32[768]{0:T(1024)S(1)} %copy-done.50), kind=kOutput, calls=%fused_computation.70 | convolution fusion | flops 3701182464 | bytes 13151232 | tf_op jit(solution)/shard_map/rtf,tdf->rd/dot_general | solution.py:97
  385.9 9.8 %all-gather.7.cloned.1.call-done = f32[294912]{0:T(1024)} async-done(((f32[9216]{0:T(1024)}), f32[294912]{0:T(1024)}) %all-gather.7.cloned.1.call-update) | async-done | bytes 1179664 | tf_op jit(solution)/shard_map/all_gather | solution.py:175
  395.8 1.4 reshape.273
  397.9 165.6 %reduce-scatter.2.cloned.1.call-done = bf16[1,3,96,768]{3,2,1,0:T(8,128)(2,1)} async-done(((bf16[32,3,96,768]{3,2,1,0:T(8,128)(2,1)}), bf16[1,3,96,768]{3,2,1,0:T(8,128)(2,1)}) %reduce-scatter.2.cloned.1.call-update) | async-done | bytes 442384 | tf_op jit(solution)/shard_map/reduce_scatter | solution.py:58
  563.6 1.1 convert_element_type.148
  (174 shorter events, 12.9 us)
Async XLA Ops:
  7.2 8.9 %copy-start.3 = (bf16[784,768]{1,0:T(8,128)(2,1)S(1)}, bf16[784,768]{1,0:T(8,128)(2,1)}, u32[]{:S(2)}) copy-start(bf16[784,768]{1,0:T(8,128)(2,1)} %param.14) | copy-start | bytes 3612676
  7.2 110.3 %all-gather.5.cloned.1.call-start = ((), (), s32[]{:S(2)}) async-start(), calls=%async_computation.2 | async-start | bytes 14598144 | tf_op jit(solution)/shard_map/all_gather | solution.py:47
  11.0 384.7 %all-gather.7.cloned.1.call-start = ((), (), s32[]{:S(2)}) async-start(), calls=%async_computation.3 | async-start | bytes 1216512 | tf_op jit(solution)/shard_map/all_gather | solution.py:175
  15.1 109.3 %copy-start.39 = (f32[768]{0:T(1024)}, f32[768]{0:T(1024)S(1)}, u32[]{:S(2)}) copy-start(f32[768]{0:T(1024)S(1)} %get-tuple-element.105) | copy-start | bytes 9220
  15.1 109.3 %copy-start.53 = (f32[768]{0:T(1024)}, f32[768]{0:T(1024)S(1)}, u32[]{:S(2)}) copy-start(f32[768]{0:T(1024)S(1)} %get-tuple-element.104) | copy-start | bytes 9220
  15.1 177.6 %copy-start.51 = (f32[768]{0:T(1024)}, f32[768]{0:T(1024)S(1)}, u32[]{:S(2)}) copy-start(f32[768]{0:T(1024)S(1)} %get-tuple-element.99) | copy-start | bytes 9220
  15.1 198.5 %copy-start.41 = (f32[768]{0:T(1024)}, f32[768]{0:T(1024)S(1)}, u32[]{:S(2)}) copy-start(f32[768]{0:T(1024)S(1)} %get-tuple-element.100) | copy-start | bytes 9220
  15.2 139.4 %copy-start.29 = (f32[12,64]{1,0:T(8,128)}, f32[12,64]{1,0:T(8,128)S(1)}, u32[]{:S(2)}) copy-start(f32[12,64]{1,0:T(8,128)S(1)} %add.135) | copy-start | bytes 9220
  16.3 108.2 %copy-start.32 = (f32[784]{0:T(1024)}, f32[784]{0:T(1024)S(1)}, u32[]{:S(2)}) copy-start(f32[784]{0:T(1024)S(1)} %broadcast_multiply_fusion.5) | copy-start | bytes 9412
  16.8 107.6 %copy-start.43 = (f32[784]{0:T(1024)}, f32[784]{0:T(1024)S(1)}, u32[]{:S(2)}) copy-start(f32[784]{0:T(1024)S(1)} %add_rsqrt_fusion.1) | copy-start | bytes 9412
  123.7 6.6 %copy-start.11 = (bf16[1,4,8,96,768]{4,3,2,1,0:T(8,128)(2,1)}, bf16[1,4,8,96,768]{4,3,2,1,0:T(8,128)(2,1)S(1)}, u32[]{:S(2)}) copy-start(bf16[1,4,8,96,768]{4,3,2,1,0:T(8,128)(2,1)S(1)} %copy.98) | copy-start | bytes 14155780
  150.0 4.6 copy-start
  150.1 4.6 copy-start.20
  173.5 14.8 %copy-start.4 = (bf16[784,768]{1,0:T(8,128)(2,1)S(1)}, bf16[784,768]{1,0:T(8,128)(2,1)}, u32[]{:S(2)}) copy-start(bf16[784,768]{1,0:T(8,128)(2,1)} %param.14) | copy-start | bytes 3612676
  188.3 4.5 slice-start.2
  188.3 4.5 slice-start.3
  188.3 11.0 %slice-start = ((s8[4718592]{0:T(1024)(128)(4,1)}), s8[4194304]{0:T(1024)(128)(4,1)S(1)}, s32[]{:S(2)}) async-start(s8[4718592]{0:T(1024)(128)(4,1)} %bitcast.168), calls=%async_computation.4 | async-start | bytes 8388608
  192.2 21.4 %copy-start.9 = (f32[784,768]{1,0:T(8,128)}, f32[784,768]{1,0:T(8,128)S(1)}, u32[]{:S(2)}) copy-start(f32[784,768]{1,0:T(8,128)S(1)} %get-tuple-element.109) | copy-start | bytes 7225348
  192.2 21.4 %copy-start.34 = (f32[784]{0:T(1024)}, f32[784]{0:T(1024)S(1)}, u32[]{:S(2)}) copy-start(f32[784]{0:T(1024)S(1)} %broadcast_multiply_fusion.4) | copy-start | bytes 9412
  192.7 20.9 %copy-start.45 = (f32[784]{0:T(1024)}, f32[784]{0:T(1024)S(1)}, u32[]{:S(2)}) copy-start(f32[784]{0:T(1024)S(1)} %add_rsqrt_fusion) | copy-start | bytes 9412
  192.8 6.5 %slice-start.1 = ((s8[4718592]{0:T(1024)(128)(4,1)}), s8[524288]{0:T(1024)(128)(4,1)S(1)}, s32[]{:S(2)}) async-start(s8[4718592]{0:T(1024)(128)(4,1)} %bitcast.168), calls=%async_computation.5 | async-start | bytes 1048576
  192.8 6.5 %copy-start.17 = (bf16[784,768]{1,0:T(8,128)(2,1)S(1)}, bf16[784,768]{1,0:T(8,128)(2,1)}, u32[]{:S(2)}) copy-start(bf16[784,768]{1,0:T(8,128)(2,1)} %param.15) | copy-start | bytes 3612676
  208.7 4.9 copy-start.57
  220.6 15.0 %copy-start.13 = (f32[784,4,192]{0,2,1:T(8,128)S(1)}, f32[784,4,192]{0,2,1:T(8,128)}, u32[]{:S(2)}) copy-start(f32[784,4,192]{0,2,1:T(8,128)} %copy.100) | copy-start | bytes 7225348
  261.3 27.9 %copy-start.1 = (f32[784,4,192]{0,2,1:T(8,128)S(1)}, f32[784,4,192]{0,2,1:T(8,128)}, u32[]{:S(2)}) copy-start(f32[784,4,192]{0,2,1:T(8,128)} %copy-done) | copy-start | bytes 7225348
  261.3 27.9 %copy-start.30 = (f32[12,64]{1,0:T(8,128)S(1)}, f32[12,64]{1,0:T(8,128)}, u32[]{:S(2)}) copy-start(f32[12,64]{1,0:T(8,128)} %copy-done.29) | copy-start | bytes 9220
  289.1 10.0 %copy-start.12 = (bf16[784,4,192]{0,2,1:T(8,128)(2,1)S(1)}, bf16[784,4,192]{0,2,1:T(8,128)(2,1)}, u32[]{:S(2)}) copy-start(bf16[784,4,192]{0,2,1:T(8,128)(2,1)} %copy.102) | copy-start | bytes 3612676
  311.9 4.5 copy-start.5
  311.9 4.5 copy-start.33
  311.9 4.4 copy-start.40
  311.9 4.4 copy-start.44
  316.4 8.4 %copy-start.15 = (bf16[784,4,192]{2,0,1:T(8,128)(2,1)S(1)}, bf16[784,4,192]{2,0,1:T(8,128)(2,1)}, u32[]{:S(2)}) copy-start(bf16[784,4,192]{2,0,1:T(8,128)(2,1)} %copy.111) | copy-start | bytes 3612676
  316.4 8.4 %copy-start.16 = (bf16[784,4,192]{2,0,1:T(8,128)(2,1)S(1)}, bf16[784,4,192]{2,0,1:T(8,128)(2,1)}, u32[]{:S(2)}) copy-start(bf16[784,4,192]{2,0,1:T(8,128)(2,1)} %copy.110) | copy-start | bytes 3612676
  316.4 8.4 %copy-start.54 = (f32[768]{0:T(1024)S(1)}, f32[768]{0:T(1024)}, u32[]{:S(2)}) copy-start(f32[768]{0:T(1024)} %copy-done.53) | copy-start | bytes 9220
  324.8 6.8 %copy-start.18 = (bf16[784,768]{1,0:T(8,128)(2,1)S(1)}, bf16[784,768]{1,0:T(8,128)(2,1)}, u32[]{:S(2)}) copy-start(bf16[784,768]{1,0:T(8,128)(2,1)} %param.15) | copy-start | bytes 3612676
  331.6 9.2 %copy-start.49 = (f32[4,768]{1,0:T(4,128)S(1)}, f32[4,768]{1,0:T(4,128)}, u32[]{:S(2)}) copy-start(f32[4,768]{1,0:T(4,128)} %get-tuple-element.120) | copy-start | bytes 36868
  343.4 6.0 %copy-start.35 = (f32[784]{0:T(1024)S(1)}, f32[784]{0:T(1024)}, u32[]{:S(2)}) copy-start(f32[784]{0:T(1024)} %copy-done.34) | copy-start | bytes 9412
  343.4 6.0 %copy-start.42 = (f32[768]{0:T(1024)S(1)}, f32[768]{0:T(1024)}, u32[]{:S(2)}) copy-start(f32[768]{0:T(1024)} %copy-done.41) | copy-start | bytes 9220
  343.4 6.0 %copy-start.46 = (f32[784]{0:T(1024)S(1)}, f32[784]{0:T(1024)}, u32[]{:S(2)}) copy-start(f32[784]{0:T(1024)} %copy-done.45) | copy-start | bytes 9412
  343.4 6.0 %copy-start.52 = (f32[768]{0:T(1024)S(1)}, f32[768]{0:T(1024)}, u32[]{:S(2)}) copy-start(f32[768]{0:T(1024)} %copy-done.51) | copy-start | bytes 9220
  343.4 220.1 %reduce-scatter.2.cloned.1.call-start = ((), (), s32[]{:S(2)}) async-start(), calls=%async_computation.1 | async-start | bytes 14598144 | tf_op jit(solution)/shard_map/reduce_scatter | solution.py:58
  349.4 8.5 %copy-start.2 = (bf16[4,768,576]{2,1,0:T(8,128)(2,1)S(1)}, bf16[4,768,576]{2,1,0:T(8,128)(2,1)}, u32[]{:S(2)}) copy-start(bf16[4,768,576]{2,1,0:T(8,128)(2,1)} %copy.113) | copy-start | bytes 10616836
  369.4 3.1 copy-start.22
  369.5 3.8 copy-start.28
  369.5 3.8 copy-start.36
  370.2 3.6 copy-start.8
  373.9 3.3 copy-start.10
  373.9 3.3 copy-start.50
  (17 other events, 33.2 us)
Sparse Core Ops, SparseCore 0:
  11.5 105.9 all-gather.4
  343.5 52.2 all-gather.6
  401.8 161.7 reduce-scatter.1
